TPU v7x, 32 devices: a whole 2x2x4 slice. The times are simulated.
32 devices in a mesh: gx: 4 (over x, core), gy: 4 (over z), gz: 2 (over y).
Axes of the slice: x: 2, y: 2, z: 4, core: 2. Of those that a mesh axis runs over, the one named last changes fastest.
Arguments:
- loads: bfloat16 [4, 4, 2, 2048, 128], P('gx', 'gy', 'gz'), may hold values from -12 to 12, as said below
- start_guess: bfloat16 [4, 4, 2, 2048, 128], P('gx', 'gy', 'gz'), may hold values from -1.1953125 to 1.1953125
- schur_blocks: bfloat16 [4, 4, 2, 2048, 2048], P('gx', 'gy', 'gz'), may hold values from -1 to 5, as said below
- coupling: bfloat16 [4, 4, 2, 6, 128, 128], P('gx', 'gy', 'gz'), may hold values from -0.25 to 0.25
- diag_inverse: bfloat16 [4, 4, 2, 16, 128, 128], P('gx', 'gy', 'gz'), may hold values from -1 to 1, as said below
- lower_blocks: bfloat16 [4, 4, 2, 15, 128, 128], P('gx', 'gy', 'gz'), may hold values from -0.1875 to 0.1875
- upper_blocks: bfloat16 [4, 4, 2, 15, 128, 128], P('gx', 'gy', 'gz'), may hold values from -0.1875 to 0.1875
Outputs:
- solution: float32 [4, 4, 2, 2048, 128], P('gx', 'gy', 'gz')
- residual_ratio: float32 [128], replicated
Inputs may be any that keep to these rules, and one draw needn't show every extreme that they name: Each subdomain's loads are independent entries times a factor of that subdomain. `schur_blocks`: each subdomain's Schur block has a positive diagonal between 2 and 4 and full independent off-diagonal entries. `diag_inverse`: each block has a positive diagonal between 0.25 and 0.5 and full independent off-diagonal entries.
All inputs are finite; a program needn't handle non-finite values.
Results may differ from a plain program's by a relative error of at most 0.0037.
Values may be sent and summed in bfloat16 or wider, within the bound.
A program may use at most 64 MiB of HBM per device.

v0:
```python
import jax
import jax.numpy as jnp
from jax import lax
from jax.sharding import PartitionSpec as P

U = 2048
F = 128
B = 128
R = 128
ITERS = 2
NB = 16
epsilon = 1e-06


def with_halo(cells, sides, width):
    for axis, dim in sides:
        count = lax.axis_size(axis)
        head = lax.slice_in_dim(cells, 0, width, axis=dim)
        tail = lax.slice_in_dim(cells, cells.shape[dim] - width, cells.shape[dim], axis=dim)
        cells = jnp.concatenate(
            [
                lax.ppermute(tail, axis, [(i, (i + 1) % count) for i in range(count)]),
                cells,
                lax.ppermute(head, axis, [((i + 1) % count, i) for i in range(count)]),
            ],
            axis=dim,
        )
    return cells


def neighbour_faces(face_rows):
    along_x = with_halo(face_rows[0:2][None], (("gx", 0),), 1)
    along_y = with_halo(face_rows[2:4][None], (("gy", 0),), 1)
    along_z = with_halo(face_rows[4:6][None], (("gz", 0),), 1)
    return jnp.stack(
        [along_x[0, 1], along_x[2, 0], along_y[0, 1], along_y[2, 0], along_z[0, 1], along_z[2, 0]]
    )


def operate(values, schur_block, couple_block):
    own_part = jnp.dot(schur_block, values, preferred_element_type=jnp.float32)
    face_rows = values[: 6 * F].reshape(6, F, values.shape[1])
    neighbours = neighbour_faces(face_rows)
    coupled = lax.dot_general(
        couple_block, neighbours, (((2,), (1,)), ((0,), (0,))), preferred_element_type=jnp.float32
    )
    return jnp.concatenate(
        [own_part[: 6 * F] + coupled.reshape(6 * F, R), own_part[6 * F :]], axis=0
    )


def precondition(values, diag_blocks, lower_one, upper_one):
    blocks = values.reshape(NB, B, R)

    def forward(previous, inputs):
        block_in, lower_block = inputs
        current = block_in - jnp.dot(
            lower_block, previous.astype(jnp.bfloat16), preferred_element_type=jnp.float32
        )
        return (current, current)

    carried, remaining = lax.scan(forward, blocks[0], (blocks[1:], lower_one))
    forward_sweep = jnp.concatenate([blocks[0][None], remaining], axis=0)
    final_block = jnp.dot(
        diag_blocks[NB - 1],
        forward_sweep[NB - 1].astype(jnp.bfloat16),
        preferred_element_type=jnp.float32,
    )

    def backward(next_block, inputs):
        block_in, diag_block, upper_block = inputs
        inner = block_in - jnp.dot(
            upper_block, next_block.astype(jnp.bfloat16), preferred_element_type=jnp.float32
        )
        current = jnp.dot(
            diag_block, inner.astype(jnp.bfloat16), preferred_element_type=jnp.float32
        )
        return (current, current)

    carried, earlier = lax.scan(
        backward, final_block, (forward_sweep[:-1], diag_blocks[:-1], upper_one), reverse=True
    )
    return jnp.concatenate([earlier, final_block[None]], axis=0).reshape(U, R)


def least_squares(hessenberg, start_norm):
    columns = hessenberg.shape[1]
    unit_vectors = []
    triangle = {}
    for column in range(columns):
        vector = hessenberg[:, column]
        for earlier in range(column):
            weight = jnp.sum(unit_vectors[earlier] * vector, axis=0)
            triangle[earlier, column] = weight
            vector = vector - weight * unit_vectors[earlier]
        length = jnp.sqrt(jnp.sum(vector * vector, axis=0))
        triangle[column, column] = length
        unit_vectors.append(vector / length)
    target = [start_norm * unit_vectors[column][0] for column in range(columns)]
    coeffs = [None] * columns
    for column in range(columns - 1, -1, -1):
        running = target[column]
        for earlier in range(column + 1, columns):
            running = running - triangle[column, earlier] * coeffs[earlier]
        coeffs[column] = running / triangle[column, column]
    coeffs = jnp.stack(coeffs)
    unit_first = jnp.zeros((columns + 1, 1), jnp.float32).at[0].set(1.0)
    misfit = unit_first * start_norm - jnp.sum(hessenberg * coeffs[None], axis=1)
    return (coeffs, jnp.sqrt(jnp.sum(misfit * misfit, axis=0)) / start_norm)


def body(loads, start_guess, schur_blocks, coupling, diag_inverse, lower_blocks, upper_blocks):
    schur_block = schur_blocks[0, 0, 0]
    couple_block = coupling[0, 0, 0]
    diag_blocks = diag_inverse[0, 0, 0]
    lower_one = lower_blocks[0, 0, 0]
    upper_one = upper_blocks[0, 0, 0]
    warm_start = start_guess[0, 0, 0]
    residual = loads[0, 0, 0].astype(jnp.float32) - operate(warm_start, schur_block, couple_block)
    start_norm = jnp.sqrt(
        lax.psum(jnp.sum(residual * residual, axis=0), ("gx", "gy", "gz")) + epsilon
    )
    krylov = [residual / start_norm]
    hessenberg = jnp.zeros((ITERS + 1, ITERS, R), jnp.float32)
    directions = []
    for column in range(ITERS):
        direction = precondition(krylov[column], diag_blocks, lower_one, upper_one)
        directions.append(direction)
        mapped = operate(direction.astype(jnp.bfloat16), schur_block, couple_block)
        stacked = jnp.stack(krylov)
        own_products = jnp.sum(stacked * mapped[None], axis=1)
        projected, squares = lax.psum(
            (own_products, jnp.sum(mapped * mapped, axis=0)), ("gx", "gy", "gz")
        )
        mapped = mapped - jnp.sum(projected[:, None, :] * stacked, axis=0)
        length = jnp.sqrt(squares - jnp.sum(projected * projected, axis=0) + epsilon)
        hessenberg = (
            hessenberg.at[: column + 1, column].set(projected).at[column + 1, column].set(length)
        )
        if column + 1 < ITERS:
            krylov.append(mapped / length)
    coeffs, residual_ratio = least_squares(hessenberg, start_norm)
    solution = warm_start.astype(jnp.float32)
    for column in range(ITERS):
        solution = solution + coeffs[column] * directions[column]
    return (solution[None, None, None], residual_ratio)


def solution(mesh):
    in_specs = (
        P("gx", "gy", "gz", None, None),
        P("gx", "gy", "gz", None, None),
        P("gx", "gy", "gz", None, None),
        P("gx", "gy", "gz", None, None, None),
        P("gx", "gy", "gz", None, None, None),
        P("gx", "gy", "gz", None, None, None),
        P("gx", "gy", "gz", None, None, None),
    )
    out_specs = (P("gx", "gy", "gz", None, None), P())
    return jax.shard_map(body, mesh=mesh, in_specs=in_specs, out_specs=out_specs, check_vma=False)
```

profile of v0, /device:TPU:0, one launch (start us, length us, event | category | flops | bytes accessed | tf_op | source)
XLA Modules:
  0.0 269.4 jit_solution(9059985981006871884)
XLA Ops:
  2.2 2.0 collective-permute-start.1
  4.2 2.3 collective-permute-start.2
  6.5 2.0 collective-permute-start.3
  10.3 5.8 %fusion.40 = f32[2048,128]{1,0:T(8,128)S(1)} fusion(bf16[1,1,1,2048,2048]{4,3,2,1,0:T(8,128)(2,1)} %param.27, bf16[1,1,1,2048,128]{4,3,2,1,0:T(8,128)(2,1)} %param.26), kind=kOutput, calls=%fused_computation.40 | convolution fusion | flops 1073741824 | bytes 9961472 | tf_op jit(solution)/shard_map/dot_general | solution.py:41
  18.9 3.9 %collective-permute-done.5 = bf16[1,2,128,128]{3,2,1,0:T(8,128)(2,1)S(1)} collective-permute-done((bf16[1,2,128,128]{3,2,1,0:T(8,128)(2,1)S(1)}, bf16[1,2,128,128]{3,2,1,0:T(8,128)(2,1)S(1)}, u32[]{:S(2)}, u32[]{:S(2)}) %collective-permute-start.5) | collective-permute-done | bytes 65568 | tf_op jit(solution)/shard_map/ppermute | solution.py:24
  23.4 37.7 %psum.35 = f32[128]{0:T(128)S(1)} all-reduce(f32[128]{0:T(128)S(1)} %multiply_reduce_fusion.3), channel_id=1, replica_groups=mesh['gx'=4,'gy'=4,'gz'=2] {'gx','gy','gz'}, use_global_device_ids=true, to_apply=%region_1.0 | all-reduce | flops 128 | bytes 1024 | tf_op jit(solution)/shard_map/psum | solution.py:121
  63.4 15.6 %while.61 = (s32[]{:T(128)}, bf16[128,128]{1,0:T(8,128)(2,1)S(1)}, f32[15,128,128]{2,1,0:T(8,128)S(1)}, f32[15,128,128]{2,1,0:T(8,128)}, bf16[15,128,128]{2,1,0:T(8,128)(2,1)}, /*index=5*/s32[]{:T(128)}) while((s32[]{:T(128)}, bf16[128,128]{1,0:T(8,128)(2,1)S(1)}, f32[15,128,128]{2,1,0:T(8,128)S(1)}, f32[15,128,128]{2,1,0:T(8,128)}, ...), condition=%wide.region_3.4_spmd, body=%wide.region_2.3_spmd.sunk | while | flops 4227074 | bytes 296005 | solution.py:62
  81.0 18.0 %while.62 = (s32[]{:T(128)}, bf16[128,128]{1,0:T(8,128)(2,1)S(1)}, f32[15,128,128]{2,1,0:T(8,128)S(1)}, bf16[15,128,128]{2,1,0:T(8,128)(2,1)}, f32[15,128,128]{2...) while((s32[]{:T(128)}, bf16[128,128]{1,0:T(8,128)(2,1)S(1)}, ...), condition=%wide.region_5.6_spmd, body=%wide.region_4.5_spmd.sunk | while | flops 8437763 | bytes 329825 | solution.py:80
  100.9 2.0 collective-permute-start.8
  102.8 1.9 collective-permute-start.9
  104.7 5.9 %fusion.42 = f32[2048,128]{1,0:T(8,128)S(1)} fusion(bf16[2048,128]{1,0:T(8,128)(2,1)S(1)} %bitcast.335, bf16[1,1,1,2048,2048]{4,3,2,1,0:T(8,128)(2,1)} %param.27), kind=kOutput, calls=%fused_computation.42 | convolution fusion | flops 1073741824 | bytes 9961472 | tf_op jit(solution)/shard_map/dot_general | solution.py:41
  111.8 2.3 collective-permute-start.10
  114.2 2.8 %collective-permute-done.10 = bf16[1,2,128,128]{3,2,1,0:T(8,128)(2,1)S(1)} collective-permute-done((bf16[1,2,128,128]{3,2,1,0:T(8,128)(2,1)S(1)}, bf16[1,2,128,128]{3,2,1,0:T(8,128)(2,1)S(1)}, u32[]{:S(2)}, u32[]{:S(2)}) %collective-permute-start.10) | collective-permute-done | bytes 65568 | tf_op jit(solution)/shard_map/ppermute | solution.py:22
  119.2 38.1 %all-reduce.2 = (f32[128]{0:T(128)S(1)}, f32[1,128]{1,0:T(1,128)S(1)}) all-reduce(f32[128]{0:T(128)S(1)} %multiply_reduce_fusion.1, f32[1,128]{1,0:T(1,128)S(1)} %bitcast.351), channel_id=1, replica_groups=mesh['gx'=4,'gy'=4,'gz'=2] {'gx','gy','gz'}, use_global_device_ids=true, to_apply=%region_9.10 | all-reduce | flops 256 | bytes 2048 | tf_op jit(solution)/shard_map/psum | solution.py:132
  159.7 15.6 %while.63 = (s32[]{:T(128)}, bf16[128,128]{1,0:T(8,128)(2,1)S(1)}, f32[15,128,128]{2,1,0:T(8,128)S(1)}, f32[15,128,128]{2,1,0:T(8,128)}, bf16[15,128,128]{2,1,0:T(8,128)(2,1)}, /*index=5*/s32[]{:T(128)}) while((s32[]{:T(128)}, bf16[128,128]{1,0:T(8,128)(2,1)S(1)}, f32[15,128,128]{2,1,0:T(8,128)S(1)}, f32[15,128,128]{2,1,0:T(8,128)}, ...), condition=%wide.region_11.12_spmd, body=%wide.region_10.11_spmd.sunk | while | flops 4227074 | bytes 296005 | solution.py:62
  177.3 18.0 %while.64 = (s32[]{:T(128)}, bf16[128,128]{1,0:T(8,128)(2,1)S(1)}, f32[15,128,128]{2,1,0:T(8,128)S(1)}, bf16[15,128,128]{2,1,0:T(8,128)(2,1)}, f32[15,128,128]{2...) while((s32[]{:T(128)}, bf16[128,128]{1,0:T(8,128)(2,1)S(1)}, ...), condition=%wide.region_13.14_spmd, body=%wide.region_12.13_spmd.sunk | while | flops 8437763 | bytes 329825 | solution.py:80
  196.0 1.7 collective-permute-start.13
  197.7 1.8 collective-permute-start.14
  199.5 2.0 collective-permute-start.15
  202.6 2.3 collective-permute-start.16
  206.0 6.4 %fusion.45 = f32[2048,128]{0,1:T(8,128)S(1)} fusion(bf16[2048,128]{1,0:T(8,128)(2,1)S(1)} %bitcast.327, bf16[1,1,1,2048,2048]{4,3,2,1,0:T(8,128)(2,1)} %param.27), kind=kOutput, calls=%fused_computation.43 | convolution fusion | flops 1073741824 | bytes 9961472 | tf_op jit(solution)/shard_map/dot_general | solution.py:41
  218.7 1.9 copy.18
  225.8 38.7 %all-reduce.1 = (f32[2,128]{1,0:T(2,128)S(1)}, f32[128]{0:T(128)S(1)}) all-reduce(f32[2,128]{1,0:T(2,128)S(1)} %fusion.48, f32[128]{0:T(128)S(1)} %get-tuple-element.426), channel_id=1, replica_groups=mesh['gx'=4,'gy'=4,'gz'=2] {'gx','gy','gz'}, use_global_device_ids=true, to_apply=%region_15.16 | all-reduce | flops 384 | bytes 3072 | tf_op jit(solution)/shard_map/psum | solution.py:132
  266.6 2.8 %multiply_add_fusion = f32[1,1,1,2048,128]{4,3,2,1,0:T(8,128)} fusion(f32[1,1,1,2048,128]{4,3,2,1,0:T(8,128)} %bitcast.326, f32[1,1,1,2048,128]{4,3,2,1,0:T(8,128)} %bitcast.325, bf16[1,1,1,2048,128]{4,3,2,1,0:T(8,128)(2,1)} %param.26, f32[128]{0:T(128)S(1)} %get-tuple-element.413, f32[128]{0:T(128)S(1)} %get-tuple-element.412), kind=kLoop, calls=%fused_computation.56 | loop fusion | flops 1310720 | bytes 3671040 | tf_op jit(solution)/shard_map/add | solution.py:145
  (244 shorter events, 102.3 us)
Async XLA Ops:
  0.6 22.2 %copy-start = (bf16[1,1,1,6,128,128]{5,4,3,2,1,0:T(8,128)(2,1)S(1)}, bf16[1,1,1,6,128,128]{5,4,3,2,1,0:T(8,128)(2,1)}, u32[]{:S(2)}) copy-start(bf16[1,1,1,6,128,128]{5,4,3,2,1,0:T(8,128)(2,1)} %param.28) | copy-start | bytes 589828
  0.6 16.4 %copy-start.8 = (bf16[1,1,1,16,128,128]{5,4,3,2,1,0:T(8,128)(2,1)S(1)}, bf16[1,1,1,16,128,128]{5,4,3,2,1,0:T(8,128)(2,1)}, u32[]{:S(2)}) copy-start(bf16[1,1,1,16,128,128]{5,4,3,2,1,0:T(8,128)(2,1)} %param.29) | copy-start | bytes 1572868
  0.7 22.4 %copy-start.4 = (bf16[1,1,1,2048,128]{4,3,2,1,0:T(8,128)(2,1)S(1)}, bf16[1,1,1,2048,128]{4,3,2,1,0:T(8,128)(2,1)}, u32[]{:S(2)}) copy-start(bf16[1,1,1,2048,128]{4,3,2,1,0:T(8,128)(2,1)} %param.25) | copy-start | bytes 1572868
  1.7 16.9 %collective-permute-start = (bf16[1,2,128,128]{3,2,1,0:T(8,128)(2,1)S(1)}, bf16[1,2,128,128]{3,2,1,0:T(8,128)(2,1)S(1)}, u32[]{:S(2)}, u32[]{:S(2)}) collective-permute-start(bf16[1,2,128,128]{3,2,1,0:T(8,128)(2,1)S(1)} %bitcast.342), channel_id=1, source_target_pairs={{0,8},{8,16},{16,24},{24,0},{1,9},{9,17},{17,25},{25,1},{2,10},{10... | collective-permute-start | bytes 196616 | tf_op jit(solution)/shard_map/ppermute | solution.py:22
  2.2 16.6 %collective-permute-start.1 = (bf16[1,2,128,128]{3,2,1,0:T(8,128)(2,1)S(1)}, bf16[1,2,128,128]{3,2,1,0:T(8,128)(2,1)S(1)}, u32[]{:S(2)}, u32[]{:S(2)}) collective-permute-start(bf16[1,2,128,128]{3,2,1,0:T(8,128)(2,1)S(1)} %bitcast.343), channel_id=1, source_target_pairs={{8,0},{16,8},{24,16},{0,24},{9,1},{17,9},{25,17},{1,25},{10,2},{18... | collective-permute-start | bytes 196616 | tf_op jit(solution)/shard_map/ppermute | solution.py:24
  4.2 14.6 %collective-permute-start.2 = (bf16[1,2,128,128]{3,2,1,0:T(8,128)(2,1)S(1)}, bf16[1,2,128,128]{3,2,1,0:T(8,128)(2,1)S(1)}, u32[]{:S(2)}, u32[]{:S(2)}) collective-permute-start(bf16[1,2,128,128]{3,2,1,0:T(8,128)(2,1)S(1)} %bitcast.340), channel_id=1, source_target_pairs={{0,2},{2,4},{4,6},{6,0},{1,3},{3,5},{5,7},{7,1},{8,10},{10,12},{12... | collective-permute-start | bytes 196616 | tf_op jit(solution)/shard_map/ppermute | solution.py:22
  6.5 12.3 %collective-permute-start.3 = (bf16[1,2,128,128]{3,2,1,0:T(8,128)(2,1)S(1)}, bf16[1,2,128,128]{3,2,1,0:T(8,128)(2,1)S(1)}, u32[]{:S(2)}, u32[]{:S(2)}) collective-permute-start(bf16[1,2,128,128]{3,2,1,0:T(8,128)(2,1)S(1)} %bitcast.341), channel_id=1, source_target_pairs={{2,0},{4,2},{6,4},{0,6},{3,1},{5,3},{7,5},{1,7},{10,8},{12,10},{14... | collective-permute-start | bytes 196616 | tf_op jit(solution)/shard_map/ppermute | solution.py:24
  8.6 10.3 %collective-permute-start.4 = (bf16[1,2,128,128]{3,2,1,0:T(8,128)(2,1)S(1)}, bf16[1,2,128,128]{3,2,1,0:T(8,128)(2,1)S(1)}, u32[]{:S(2)}, u32[]{:S(2)}) collective-permute-start(bf16[1,2,128,128]{3,2,1,0:T(8,128)(2,1)S(1)} %bitcast.338), channel_id=1, source_target_pairs={{0,1},{1,0},{2,3},{3,2},{4,5},{5,4},{6,7},{7,6},{8,9},{9,8},{10,11... | collective-permute-start | bytes 196616 | tf_op jit(solution)/shard_map/ppermute | solution.py:22
  18.6 4.3 %collective-permute-start.5 = (bf16[1,2,128,128]{3,2,1,0:T(8,128)(2,1)S(1)}, bf16[1,2,128,128]{3,2,1,0:T(8,128)(2,1)S(1)}, u32[]{:S(2)}, u32[]{:S(2)}) collective-permute-start(bf16[1,2,128,128]{3,2,1,0:T(8,128)(2,1)S(1)} %bitcast.339), channel_id=1, source_target_pairs={{1,0},{0,1},{3,2},{2,3},{5,4},{4,5},{7,6},{6,7},{9,8},{8,9},{11,10... | collective-permute-start | bytes 196616 | tf_op jit(solution)/shard_map/ppermute | solution.py:24
  99.1 15.0 %collective-permute-start.6 = (bf16[1,2,128,128]{3,2,1,0:T(8,128)(2,1)S(1)}, bf16[1,2,128,128]{3,2,1,0:T(8,128)(2,1)S(1)}, u32[]{:S(2)}, u32[]{:S(2)}) collective-permute-start(bf16[1,2,128,128]{3,2,1,0:T(8,128)(2,1)S(1)} %get-tuple-element.441), channel_id=1, source_target_pairs={{0,8},{8,16},{16,24},{24,0},{1,9},{9,17},{17,25},{25,1},{2,10},{10... | collective-permute-start | bytes 196616 | tf_op jit(solution)/shard_map/ppermute | solution.py:22
  99.1 14.9 %collective-permute-start.7 = (bf16[1,2,128,128]{3,2,1,0:T(8,128)(2,1)S(1)}, bf16[1,2,128,128]{3,2,1,0:T(8,128)(2,1)S(1)}, u32[]{:S(2)}, u32[]{:S(2)}) collective-permute-start(bf16[1,2,128,128]{3,2,1,0:T(8,128)(2,1)S(1)} %get-tuple-element.441), channel_id=1, source_target_pairs={{8,0},{16,8},{24,16},{0,24},{9,1},{17,9},{25,17},{1,25},{10,2},{18... | collective-permute-start | bytes 196616 | tf_op jit(solution)/shard_map/ppermute | solution.py:24
  100.9 13.2 %collective-permute-start.8 = (bf16[1,2,128,128]{3,2,1,0:T(8,128)(2,1)S(1)}, bf16[1,2,128,128]{3,2,1,0:T(8,128)(2,1)S(1)}, u32[]{:S(2)}, u32[]{:S(2)}) collective-permute-start(bf16[1,2,128,128]{3,2,1,0:T(8,128)(2,1)S(1)} %get-tuple-element.440), channel_id=1, source_target_pairs={{0,2},{2,4},{4,6},{6,0},{1,3},{3,5},{5,7},{7,1},{8,10},{10,12},{12... | collective-permute-start | bytes 196616 | tf_op jit(solution)/shard_map/ppermute | solution.py:22
  102.8 11.3 %collective-permute-start.9 = (bf16[1,2,128,128]{3,2,1,0:T(8,128)(2,1)S(1)}, bf16[1,2,128,128]{3,2,1,0:T(8,128)(2,1)S(1)}, u32[]{:S(2)}, u32[]{:S(2)}) collective-permute-start(bf16[1,2,128,128]{3,2,1,0:T(8,128)(2,1)S(1)} %get-tuple-element.440), channel_id=1, source_target_pairs={{2,0},{4,2},{6,4},{0,6},{3,1},{5,3},{7,5},{1,7},{10,8},{12,10},{14... | collective-permute-start | bytes 196616 | tf_op jit(solution)/shard_map/ppermute | solution.py:24
  111.8 5.1 %collective-permute-start.10 = (bf16[1,2,128,128]{3,2,1,0:T(8,128)(2,1)S(1)}, bf16[1,2,128,128]{3,2,1,0:T(8,128)(2,1)S(1)}, u32[]{:S(2)}, u32[]{:S(2)}) collective-permute-start(bf16[1,2,128,128]{3,2,1,0:T(8,128)(2,1)S(1)} %get-tuple-element.439), channel_id=1, source_target_pairs={{0,1},{1,0},{2,3},{3,2},{4,5},{5,4},{6,7},{7,6},{8,9},{9,8},{10,11... | collective-permute-start | bytes 196616 | tf_op jit(solution)/shard_map/ppermute | solution.py:22
  114.1 4.3 %collective-permute-start.11 = (bf16[1,2,128,128]{3,2,1,0:T(8,128)(2,1)S(1)}, bf16[1,2,128,128]{3,2,1,0:T(8,128)(2,1)S(1)}, u32[]{:S(2)}, u32[]{:S(2)}) collective-permute-start(bf16[1,2,128,128]{3,2,1,0:T(8,128)(2,1)S(1)} %get-tuple-element.439), channel_id=1, source_target_pairs={{1,0},{0,1},{3,2},{2,3},{5,4},{4,5},{7,6},{6,7},{9,8},{8,9},{11,10... | collective-permute-start | bytes 196616 | tf_op jit(solution)/shard_map/ppermute | solution.py:24
  157.3 47.5 %copy-start.2 = (f32[1,1280,128]{2,1,0:T(8,128)S(1)}, f32[1,1280,128]{2,1,0:T(8,128)}, u32[]{:S(2)}) copy-start(f32[1,1280,128]{2,1,0:T(8,128)} %copy-done.1) | copy-start | bytes 1966084
  196.0 17.4 %collective-permute-start.12 = (bf16[1,2,128,128]{3,2,1,0:T(8,128)(2,1)}, bf16[1,2,128,128]{3,2,1,0:T(8,128)(2,1)}, u32[]{:S(2)}, u32[]{:S(2)}) collective-permute-start(bf16[1,2,128,128]{3,2,1,0:T(8,128)(2,1)} %get-tuple-element.438), channel_id=1, source_target_pairs={{0,8},{8,16},{16,24},{24,0},{1,9},{9,17},{17,25},{25,1},{2,10},{10... | collective-permute-start | bytes 196616 | tf_op jit(solution)/shard_map/ppermute | solution.py:22
  196.0 18.2 %collective-permute-start.13 = (bf16[1,2,128,128]{3,2,1,0:T(8,128)(2,1)}, bf16[1,2,128,128]{3,2,1,0:T(8,128)(2,1)}, u32[]{:S(2)}, u32[]{:S(2)}) collective-permute-start(bf16[1,2,128,128]{3,2,1,0:T(8,128)(2,1)} %get-tuple-element.438), channel_id=1, source_target_pairs={{8,0},{16,8},{24,16},{0,24},{9,1},{17,9},{25,17},{1,25},{10,2},{18... | collective-permute-start | bytes 196616 | tf_op jit(solution)/shard_map/ppermute | solution.py:24
  197.7 17.3 %collective-permute-start.14 = (bf16[1,2,128,128]{3,2,1,0:T(8,128)(2,1)S(1)}, bf16[1,2,128,128]{3,2,1,0:T(8,128)(2,1)}, u32[]{:S(2)}, u32[]{:S(2)}) collective-permute-start(bf16[1,2,128,128]{3,2,1,0:T(8,128)(2,1)S(1)} %get-tuple-element.437), channel_id=1, source_target_pairs={{0,2},{2,4},{4,6},{6,0},{1,3},{3,5},{5,7},{7,1},{8,10},{10,12},{12... | collective-permute-start | bytes 196616 | tf_op jit(solution)/shard_map/ppermute | solution.py:22
  199.5 16.2 %collective-permute-start.15 = (bf16[1,2,128,128]{3,2,1,0:T(8,128)(2,1)S(1)}, bf16[1,2,128,128]{3,2,1,0:T(8,128)(2,1)}, u32[]{:S(2)}, u32[]{:S(2)}) collective-permute-start(bf16[1,2,128,128]{3,2,1,0:T(8,128)(2,1)S(1)} %get-tuple-element.437), channel_id=1, source_target_pairs={{2,0},{4,2},{6,4},{0,6},{3,1},{5,3},{7,5},{1,7},{10,8},{12,10},{14... | collective-permute-start | bytes 196616 | tf_op jit(solution)/shard_map/ppermute | solution.py:24
  202.6 13.9 %collective-permute-start.16 = (bf16[1,2,128,128]{3,2,1,0:T(8,128)(2,1)S(1)}, bf16[1,2,128,128]{3,2,1,0:T(8,128)(2,1)}, u32[]{:S(2)}, u32[]{:S(2)}) collective-permute-start(bf16[1,2,128,128]{3,2,1,0:T(8,128)(2,1)S(1)} %get-tuple-element.436), channel_id=1, source_target_pairs={{0,1},{1,0},{2,3},{3,2},{4,5},{5,4},{6,7},{7,6},{8,9},{9,8},{10,11... | collective-permute-start | bytes 196616 | tf_op jit(solution)/shard_map/ppermute | solution.py:22
  206.0 18.2 %copy-start.6 = (f32[1,2048,128]{2,1,0:T(8,128)S(1)}, f32[1,2048,128]{2,1,0:T(8,128)}, u32[]{:S(2)}) copy-start(f32[1,2048,128]{2,1,0:T(8,128)} %subtract_divide_fusion.1) | copy-start | bytes 3145732
  212.4 53.5 %copy-start.9 = (f32[3]{0:T(128)S(1)}, f32[3]{0:T(128)}, u32[]{:S(2)}) copy-start(f32[3]{0:T(128)} %constant.255.clone.1) | copy-start | bytes 40
  213.4 4.3 %collective-permute-start.17 = (bf16[1,2,128,128]{3,2,1,0:T(8,128)(2,1)S(1)}, bf16[1,2,128,128]{3,2,1,0:T(8,128)(2,1)S(1)}, u32[]{:S(2)}, u32[]{:S(2)}) collective-permute-start(bf16[1,2,128,128]{3,2,1,0:T(8,128)(2,1)S(1)} %get-tuple-element.436), channel_id=1, source_target_pairs={{1,0},{0,1},{3,2},{2,3},{5,4},{4,5},{7,6},{6,7},{9,8},{8,9},{11,10... | collective-permute-start | bytes 196616 | tf_op jit(solution)/shard_map/ppermute | solution.py:24
  (4 other events, 45.2 us)
where the time goes:
time: 273 us; the launch traced here: 269 us
  blocking collectives  115 us (42%)
  matrix products  86.2 us (32%)
  starting transfers between devices  24.7 us (9%)
  local copies, waits for them, and re-layouts  16.3 us (6%)
  other arithmetic  16.3 us (6%)
  waiting for transfers between devices  8.5 us (3%)
    psum x2, blocking collectives, body(): lax.psum((own_products, jnp.sum(mapped * mapped, axis=0)), ('gx', 'gy', '...  76.8 us
    psum x1, blocking collectives, body(): lax.psum(jnp.sum(residual * residual, axis=0), ('gx', 'gy', 'gz')) + epsilon  37.7 us
    dot_general x30, matrix products, backward(): jnp.dot(diag_block, inner.astype(jnp.bfloat16), preferred_element_type=jn...  34.9 us
    dot_general x30, matrix products, forward(): jnp.dot(lower_block, previous.astype(jnp.bfloat16), preferred_element_typ...  30.1 us
    dot_general x3, matrix products, operate(): own_part = jnp.dot(schur_block, values, preferred_element_type=jnp.float32)  18.1 us
    ppermute x9, starting transfers between devices, with_halo(): lax.ppermute(tail, axis, [(i, (i + 1) % count) for i in range(count)])  13 us
    ppermute x9, starting transfers between devices, with_halo(): lax.ppermute(head, axis, [((i + 1) % count, i) for i in range(count)])  11.7 us
    ppermute x9, waiting for transfers between devices, with_halo(): lax.ppermute(head, axis, [((i + 1) % count, i) for i in range(count)])  5.72 us
  transfers between devices with their start and end apart: 18, of which 4 were waited for; matrix products, arithmetic and copies ran while one was open for 11% of the time, Pallas kernels for 0%

commit v1 on v0

--- a/solution.py
+++ b/solution.py
@@ -10,6 +10,12 @@
 ITERS = 2
 NB = 16
 epsilon = 1e-06
+
+
+def gather_and_add(value, mesh_axis):
+    parts = lax.all_gather(value, mesh_axis, axis=0, tiled=False)
+    total = parts.sum(axis=0)
+    return total
 
 
 def with_halo(cells, sides, width):
@@ -118,7 +124,7 @@
     warm_start = start_guess[0, 0, 0]
     residual = loads[0, 0, 0].astype(jnp.float32) - operate(warm_start, schur_block, couple_block)
     start_norm = jnp.sqrt(
-        lax.psum(jnp.sum(residual * residual, axis=0), ("gx", "gy", "gz")) + epsilon
+        gather_and_add(jnp.sum(residual * residual, axis=0), ("gx", "gy", "gz")) + epsilon
     )
     krylov = [residual / start_norm]
     hessenberg = jnp.zeros((ITERS + 1, ITERS, R), jnp.float32)

time: 273 us -> 299 us (1.095)
  blocking collectives: 115 us -> 140 us
    all_gather x0 -> x1, blocking collectives: none -> 63.6 us  [gather_and_add(): parts = lax.all_gather(value, mesh_axis, axis=0, tiled=False)]
    psum x1 -> x0, blocking collectives: 37.7 us -> none  [body(): lax.psum(jnp.sum(residual * residual, axis=0), ('gx', 'gy', 'gz')) + epsilon]
  transfers between devices with their start and end apart: 18 -> 18, of which waited for: 4 -> 4; matrix products, arithmetic and copies ran while one was open for 11% -> 10% of each run, Pallas kernels for 0% -> 0%
where the time goes in v1:
time: 299 us; the launch traced here: 295 us
  blocking collectives  140 us (47%)
  matrix products  86.2 us (29%)
  starting transfers between devices  24.5 us (8%)
  local copies, waits for them, and re-layouts  16.5 us (6%)
  other arithmetic  16.4 us (5%)
  waiting for transfers between devices  8.5 us (3%)
    psum x2, blocking collectives, body(): lax.psum((own_products, jnp.sum(mapped * mapped, axis=0)), ('gx', 'gy', '...  76.7 us
    all_gather x1, blocking collectives, gather_and_add(): parts = lax.all_gather(value, mesh_axis, axis=0, tiled=False)  63.6 us
    dot_general x30, matrix products, backward(): jnp.dot(diag_block, inner.astype(jnp.bfloat16), preferred_element_type=jn...  34.9 us
    dot_general x30, matrix products, forward(): jnp.dot(lower_block, previous.astype(jnp.bfloat16), preferred_element_typ...  30.1 us
    dot_general x3, matrix products, operate(): own_part = jnp.dot(schur_block, values, preferred_element_type=jnp.float32)  18.1 us
    ppermute x9, starting transfers between devices, with_halo(): lax.ppermute(head, axis, [((i + 1) % count, i) for i in range(count)])  12.6 us
    ppermute x9, starting transfers between devices, with_halo(): lax.ppermute(tail, axis, [(i, (i + 1) % count) for i in range(count)])  11.8 us
  transfers between devices with their start and end apart: 18, of which 4 were waited for; matrix products, arithmetic and copies ran while one was open for 10% of the time, Pallas kernels for 0%

profile of v1, /device:TPU:0, one launch (start us, length us, event | category | flops | bytes accessed | tf_op | source)
XLA Modules:
  0.0 295.2 jit_solution(2482972090971689059)
XLA Ops:
  2.2 2.0 collective-permute-start.1
  4.2 2.3 collective-permute-start.2
  6.5 2.0 collective-permute-start.3
  8.6 1.7 collective-permute-start.4
  10.3 5.8 %fusion.40 = f32[2048,128]{1,0:T(8,128)S(1)} fusion(bf16[1,1,1,2048,2048]{4,3,2,1,0:T(8,128)(2,1)} %param.27, bf16[1,1,1,2048,128]{4,3,2,1,0:T(8,128)(2,1)} %param.26), kind=kOutput, calls=%fused_computation.40 | convolution fusion | flops 1073741824 | bytes 9961472 | tf_op jit(solution)/shard_map/dot_general | solution.py:47
  18.9 3.9 %collective-permute-done.5 = bf16[1,2,128,128]{3,2,1,0:T(8,128)(2,1)S(1)} collective-permute-done((bf16[1,2,128,128]{3,2,1,0:T(8,128)(2,1)S(1)}, bf16[1,2,128,128]{3,2,1,0:T(8,128)(2,1)S(1)}, u32[]{:S(2)}, u32[]{:S(2)}) %collective-permute-start.5) | collective-permute-done | bytes 65568 | tf_op jit(solution)/shard_map/ppermute | solution.py:30
  23.4 63.6 %all-gather.1 = f32[32,1,128]{2,1,0:T(1,128)S(1)} all-gather(f32[1,1,128]{2,1,0:T(1,128)S(1)} %bitcast.364), channel_id=2, replica_groups=mesh['gx'=4,'gy'=4,'gz'=2] {'gx','gy','gz'}, dimensions={0}, use_global_device_ids=true | all-gather | bytes 16896 | tf_op jit(solution)/shard_map/all_gather | solution.py:16
  89.4 15.6 %while.61 = (s32[]{:T(128)}, bf16[128,128]{1,0:T(8,128)(2,1)S(1)}, f32[15,128,128]{2,1,0:T(8,128)S(1)}, f32[15,128,128]{2,1,0:T(8,128)}, bf16[15,128,128]{2,1,0:T(8,128)(2,1)}, /*index=5*/s32[]{:T(128)}) while((s32[]{:T(128)}, bf16[128,128]{1,0:T(8,128)(2,1)S(1)}, f32[15,128,128]{2,1,0:T(8,128)S(1)}, f32[15,128,128]{2,1,0:T(8,128)}, ...), condition=%wide.region_3.4_spmd, body=%wide.region_2.3_spmd.sunk | while | flops 4227074 | bytes 296005 | solution.py:68
  107.0 18.0 %while.62 = (s32[]{:T(128)}, bf16[128,128]{1,0:T(8,128)(2,1)S(1)}, f32[15,128,128]{2,1,0:T(8,128)S(1)}, bf16[15,128,128]{2,1,0:T(8,128)(2,1)}, f32[15,128,128]{2...) while((s32[]{:T(128)}, bf16[128,128]{1,0:T(8,128)(2,1)S(1)}, ...), condition=%wide.region_5.6_spmd, body=%wide.region_4.5_spmd.sunk | while | flops 8437763 | bytes 329825 | solution.py:86
  125.1 1.7 collective-permute-start.7
  126.8 3.8 %collective-permute-start.9 = (bf16[1,2,128,128]{3,2,1,0:T(8,128)(2,1)S(1)}, bf16[1,2,128,128]{3,2,1,0:T(8,128)(2,1)S(1)}, u32[]{:S(2)}, u32[]{:S(2)}) collective-permute-start(bf16[1,2,128,128]{3,2,1,0:T(8,128)(2,1)S(1)} %get-tuple-element.440), channel_id=1, source_target_pairs={{2,0},{4,2},{6,4},{0,6},{3,1},{5,3},{7,5},{1,7},{10,8},{12,10},{14... | collective-permute-start | bytes 196616 | tf_op jit(solution)/shard_map/ppermute | solution.py:30
  130.7 5.9 %fusion.42 = f32[2048,128]{1,0:T(8,128)S(1)} fusion(bf16[2048,128]{1,0:T(8,128)(2,1)S(1)} %bitcast.349, bf16[1,1,1,2048,2048]{4,3,2,1,0:T(8,128)(2,1)} %param.27), kind=kOutput, calls=%fused_computation.42 | convolution fusion | flops 1073741824 | bytes 9961472 | tf_op jit(solution)/shard_map/dot_general | solution.py:47
  137.8 2.0 collective-permute-start.10
  139.9 2.7 collective-permute-done.10
  145.0 37.0 %all-reduce.2 = (f32[128]{0:T(128)S(1)}, f32[1,128]{1,0:T(1,128)S(1)}) all-reduce(f32[128]{0:T(128)S(1)} %multiply_reduce_fusion.1, f32[1,128]{1,0:T(1,128)S(1)} %bitcast.366), channel_id=1, replica_groups=mesh['gx'=4,'gy'=4,'gz'=2] {'gx','gy','gz'}, use_global_device_ids=true, to_apply=%region_9.10 | all-reduce | flops 256 | bytes 2048 | tf_op jit(solution)/shard_map/psum | solution.py:138
  184.4 15.6 %while.63 = (s32[]{:T(128)}, bf16[128,128]{1,0:T(8,128)(2,1)S(1)}, f32[15,128,128]{2,1,0:T(8,128)S(1)}, f32[15,128,128]{2,1,0:T(8,128)}, bf16[15,128,128]{2,1,0:T(8,128)(2,1)}, /*index=5*/s32[]{:T(128)}) while((s32[]{:T(128)}, bf16[128,128]{1,0:T(8,128)(2,1)S(1)}, f32[15,128,128]{2,1,0:T(8,128)S(1)}, f32[15,128,128]{2,1,0:T(8,128)}, ...), condition=%wide.region_11.12_spmd, body=%wide.region_10.11_spmd.sunk | while | flops 4227074 | bytes 296005 | solution.py:68
  202.0 18.0 %while.64 = (s32[]{:T(128)}, bf16[128,128]{1,0:T(8,128)(2,1)S(1)}, f32[15,128,128]{2,1,0:T(8,128)S(1)}, bf16[15,128,128]{2,1,0:T(8,128)(2,1)}, f32[15,128,128]{2...) while((s32[]{:T(128)}, bf16[128,128]{1,0:T(8,128)(2,1)S(1)}, ...), condition=%wide.region_13.14_spmd, body=%wide.region_12.13_spmd.sunk | while | flops 8437763 | bytes 329825 | solution.py:86
  220.7 1.7 collective-permute-start.13
  222.4 2.9 collective-permute-start.14
  227.3 2.3 collective-permute-start.16
  230.7 6.4 %fusion.45 = f32[2048,128]{0,1:T(8,128)S(1)} fusion(bf16[2048,128]{1,0:T(8,128)(2,1)S(1)} %bitcast.341, bf16[1,1,1,2048,2048]{4,3,2,1,0:T(8,128)(2,1)} %param.27), kind=kOutput, calls=%fused_computation.43 | convolution fusion | flops 1073741824 | bytes 9961472 | tf_op jit(solution)/shard_map/dot_general | solution.py:47
  243.4 1.9 copy.30
  250.4 39.7 %all-reduce.1 = (f32[2,128]{1,0:T(2,128)S(1)}, f32[128]{0:T(128)S(1)}) all-reduce(f32[2,128]{1,0:T(2,128)S(1)} %fusion.48, f32[128]{0:T(128)S(1)} %get-tuple-element.426), channel_id=1, replica_groups=mesh['gx'=4,'gy'=4,'gz'=2] {'gx','gy','gz'}, use_global_device_ids=true, to_apply=%region_15.16 | all-reduce | flops 384 | bytes 3072 | tf_op jit(solution)/shard_map/psum | solution.py:138
  292.4 2.8 multiply_add_fusion
  (244 shorter events, 100.1 us)
Async XLA Ops:
  0.6 22.2 %copy-start = (bf16[1,1,1,6,128,128]{5,4,3,2,1,0:T(8,128)(2,1)S(1)}, bf16[1,1,1,6,128,128]{5,4,3,2,1,0:T(8,128)(2,1)}, u32[]{:S(2)}) copy-start(bf16[1,1,1,6,128,128]{5,4,3,2,1,0:T(8,128)(2,1)} %param.28) | copy-start | bytes 589828
  0.6 16.4 %copy-start.8 = (bf16[1,1,1,16,128,128]{5,4,3,2,1,0:T(8,128)(2,1)S(1)}, bf16[1,1,1,16,128,128]{5,4,3,2,1,0:T(8,128)(2,1)}, u32[]{:S(2)}) copy-start(bf16[1,1,1,16,128,128]{5,4,3,2,1,0:T(8,128)(2,1)} %param.29) | copy-start | bytes 1572868
  0.7 22.5 %copy-start.4 = (bf16[1,1,1,2048,128]{4,3,2,1,0:T(8,128)(2,1)S(1)}, bf16[1,1,1,2048,128]{4,3,2,1,0:T(8,128)(2,1)}, u32[]{:S(2)}) copy-start(bf16[1,1,1,2048,128]{4,3,2,1,0:T(8,128)(2,1)} %param.25) | copy-start | bytes 1572868
  1.7 16.9 %collective-permute-start = (bf16[1,2,128,128]{3,2,1,0:T(8,128)(2,1)S(1)}, bf16[1,2,128,128]{3,2,1,0:T(8,128)(2,1)S(1)}, u32[]{:S(2)}, u32[]{:S(2)}) collective-permute-start(bf16[1,2,128,128]{3,2,1,0:T(8,128)(2,1)S(1)} %bitcast.356), channel_id=1, source_target_pairs={{0,8},{8,16},{16,24},{24,0},{1,9},{9,17},{17,25},{25,1},{2,10},{10... | collective-permute-start | bytes 196616 | tf_op jit(solution)/shard_map/ppermute | solution.py:28
  2.2 16.6 %collective-permute-start.1 = (bf16[1,2,128,128]{3,2,1,0:T(8,128)(2,1)S(1)}, bf16[1,2,128,128]{3,2,1,0:T(8,128)(2,1)S(1)}, u32[]{:S(2)}, u32[]{:S(2)}) collective-permute-start(bf16[1,2,128,128]{3,2,1,0:T(8,128)(2,1)S(1)} %bitcast.357), channel_id=1, source_target_pairs={{8,0},{16,8},{24,16},{0,24},{9,1},{17,9},{25,17},{1,25},{10,2},{18... | collective-permute-start | bytes 196616 | tf_op jit(solution)/shard_map/ppermute | solution.py:30
  4.2 14.7 %collective-permute-start.2 = (bf16[1,2,128,128]{3,2,1,0:T(8,128)(2,1)S(1)}, bf16[1,2,128,128]{3,2,1,0:T(8,128)(2,1)S(1)}, u32[]{:S(2)}, u32[]{:S(2)}) collective-permute-start(bf16[1,2,128,128]{3,2,1,0:T(8,128)(2,1)S(1)} %bitcast.354), channel_id=1, source_target_pairs={{0,2},{2,4},{4,6},{6,0},{1,3},{3,5},{5,7},{7,1},{8,10},{10,12},{12... | collective-permute-start | bytes 196616 | tf_op jit(solution)/shard_map/ppermute | solution.py:28
  6.5 12.4 %collective-permute-start.3 = (bf16[1,2,128,128]{3,2,1,0:T(8,128)(2,1)S(1)}, bf16[1,2,128,128]{3,2,1,0:T(8,128)(2,1)S(1)}, u32[]{:S(2)}, u32[]{:S(2)}) collective-permute-start(bf16[1,2,128,128]{3,2,1,0:T(8,128)(2,1)S(1)} %bitcast.355), channel_id=1, source_target_pairs={{2,0},{4,2},{6,4},{0,6},{3,1},{5,3},{7,5},{1,7},{10,8},{12,10},{14... | collective-permute-start | bytes 196616 | tf_op jit(solution)/shard_map/ppermute | solution.py:30
  8.6 10.4 %collective-permute-start.4 = (bf16[1,2,128,128]{3,2,1,0:T(8,128)(2,1)S(1)}, bf16[1,2,128,128]{3,2,1,0:T(8,128)(2,1)S(1)}, u32[]{:S(2)}, u32[]{:S(2)}) collective-permute-start(bf16[1,2,128,128]{3,2,1,0:T(8,128)(2,1)S(1)} %bitcast.352), channel_id=1, source_target_pairs={{0,1},{1,0},{2,3},{3,2},{4,5},{5,4},{6,7},{7,6},{8,9},{9,8},{10,11... | collective-permute-start | bytes 196616 | tf_op jit(solution)/shard_map/ppermute | solution.py:28
  18.6 4.3 %collective-permute-start.5 = (bf16[1,2,128,128]{3,2,1,0:T(8,128)(2,1)S(1)}, bf16[1,2,128,128]{3,2,1,0:T(8,128)(2,1)S(1)}, u32[]{:S(2)}, u32[]{:S(2)}) collective-permute-start(bf16[1,2,128,128]{3,2,1,0:T(8,128)(2,1)S(1)} %bitcast.353), channel_id=1, source_target_pairs={{1,0},{0,1},{3,2},{2,3},{5,4},{4,5},{7,6},{6,7},{9,8},{8,9},{11,10... | collective-permute-start | bytes 196616 | tf_op jit(solution)/shard_map/ppermute | solution.py:30
  125.0 14.8 %collective-permute-start.6 = (bf16[1,2,128,128]{3,2,1,0:T(8,128)(2,1)S(1)}, bf16[1,2,128,128]{3,2,1,0:T(8,128)(2,1)S(1)}, u32[]{:S(2)}, u32[]{:S(2)}) collective-permute-start(bf16[1,2,128,128]{3,2,1,0:T(8,128)(2,1)S(1)} %get-tuple-element.441), channel_id=1, source_target_pairs={{0,8},{8,16},{16,24},{24,0},{1,9},{9,17},{17,25},{25,1},{2,10},{10... | collective-permute-start | bytes 196616 | tf_op jit(solution)/shard_map/ppermute | solution.py:28
  125.1 14.7 %collective-permute-start.7 = (bf16[1,2,128,128]{3,2,1,0:T(8,128)(2,1)S(1)}, bf16[1,2,128,128]{3,2,1,0:T(8,128)(2,1)S(1)}, u32[]{:S(2)}, u32[]{:S(2)}) collective-permute-start(bf16[1,2,128,128]{3,2,1,0:T(8,128)(2,1)S(1)} %get-tuple-element.441), channel_id=1, source_target_pairs={{8,0},{16,8},{24,16},{0,24},{9,1},{17,9},{25,17},{1,25},{10,2},{18... | collective-permute-start | bytes 196616 | tf_op jit(solution)/shard_map/ppermute | solution.py:30
  126.8 13.0 %collective-permute-start.8 = (bf16[1,2,128,128]{3,2,1,0:T(8,128)(2,1)S(1)}, bf16[1,2,128,128]{3,2,1,0:T(8,128)(2,1)S(1)}, u32[]{:S(2)}, u32[]{:S(2)}) collective-permute-start(bf16[1,2,128,128]{3,2,1,0:T(8,128)(2,1)S(1)} %get-tuple-element.440), channel_id=1, source_target_pairs={{0,2},{2,4},{4,6},{6,0},{1,3},{3,5},{5,7},{7,1},{8,10},{10,12},{12... | collective-permute-start | bytes 196616 | tf_op jit(solution)/shard_map/ppermute | solution.py:28
  126.8 13.0 %collective-permute-start.9 = (bf16[1,2,128,128]{3,2,1,0:T(8,128)(2,1)S(1)}, bf16[1,2,128,128]{3,2,1,0:T(8,128)(2,1)S(1)}, u32[]{:S(2)}, u32[]{:S(2)}) collective-permute-start(bf16[1,2,128,128]{3,2,1,0:T(8,128)(2,1)S(1)} %get-tuple-element.440), channel_id=1, source_target_pairs={{2,0},{4,2},{6,4},{0,6},{3,1},{5,3},{7,5},{1,7},{10,8},{12,10},{14... | collective-permute-start | bytes 196616 | tf_op jit(solution)/shard_map/ppermute | solution.py:30
  137.8 4.8 %collective-permute-start.10 = (bf16[1,2,128,128]{3,2,1,0:T(8,128)(2,1)S(1)}, bf16[1,2,128,128]{3,2,1,0:T(8,128)(2,1)S(1)}, u32[]{:S(2)}, u32[]{:S(2)}) collective-permute-start(bf16[1,2,128,128]{3,2,1,0:T(8,128)(2,1)S(1)} %get-tuple-element.439), channel_id=1, source_target_pairs={{0,1},{1,0},{2,3},{3,2},{4,5},{5,4},{6,7},{7,6},{8,9},{9,8},{10,11... | collective-permute-start | bytes 196616 | tf_op jit(solution)/shard_map/ppermute | solution.py:28
  139.8 4.3 %collective-permute-start.11 = (bf16[1,2,128,128]{3,2,1,0:T(8,128)(2,1)S(1)}, bf16[1,2,128,128]{3,2,1,0:T(8,128)(2,1)S(1)}, u32[]{:S(2)}, u32[]{:S(2)}) collective-permute-start(bf16[1,2,128,128]{3,2,1,0:T(8,128)(2,1)S(1)} %get-tuple-element.439), channel_id=1, source_target_pairs={{1,0},{0,1},{3,2},{2,3},{5,4},{4,5},{7,6},{6,7},{9,8},{8,9},{11,10... | collective-permute-start | bytes 196616 | tf_op jit(solution)/shard_map/ppermute | solution.py:30
  182.0 47.5 %copy-start.2 = (f32[1,1280,128]{2,1,0:T(8,128)S(1)}, f32[1,1280,128]{2,1,0:T(8,128)}, u32[]{:S(2)}) copy-start(f32[1,1280,128]{2,1,0:T(8,128)} %copy-done.1) | copy-start | bytes 1966084
  220.7 17.4 %collective-permute-start.12 = (bf16[1,2,128,128]{3,2,1,0:T(8,128)(2,1)}, bf16[1,2,128,128]{3,2,1,0:T(8,128)(2,1)}, u32[]{:S(2)}, u32[]{:S(2)}) collective-permute-start(bf16[1,2,128,128]{3,2,1,0:T(8,128)(2,1)} %get-tuple-element.438), channel_id=1, source_target_pairs={{0,8},{8,16},{16,24},{24,0},{1,9},{9,17},{17,25},{25,1},{2,10},{10... | collective-permute-start | bytes 196616 | tf_op jit(solution)/shard_map/ppermute | solution.py:28
  220.7 18.3 %collective-permute-start.13 = (bf16[1,2,128,128]{3,2,1,0:T(8,128)(2,1)}, bf16[1,2,128,128]{3,2,1,0:T(8,128)(2,1)}, u32[]{:S(2)}, u32[]{:S(2)}) collective-permute-start(bf16[1,2,128,128]{3,2,1,0:T(8,128)(2,1)} %get-tuple-element.438), channel_id=1, source_target_pairs={{8,0},{16,8},{24,16},{0,24},{9,1},{17,9},{25,17},{1,25},{10,2},{18... | collective-permute-start | bytes 196616 | tf_op jit(solution)/shard_map/ppermute | solution.py:30
  222.4 17.3 %collective-permute-start.14 = (bf16[1,2,128,128]{3,2,1,0:T(8,128)(2,1)S(1)}, bf16[1,2,128,128]{3,2,1,0:T(8,128)(2,1)}, u32[]{:S(2)}, u32[]{:S(2)}) collective-permute-start(bf16[1,2,128,128]{3,2,1,0:T(8,128)(2,1)S(1)} %get-tuple-element.437), channel_id=1, source_target_pairs={{0,2},{2,4},{4,6},{6,0},{1,3},{3,5},{5,7},{7,1},{8,10},{10,12},{12... | collective-permute-start | bytes 196616 | tf_op jit(solution)/shard_map/ppermute | solution.py:28
  225.3 15.2 %collective-permute-start.15 = (bf16[1,2,128,128]{3,2,1,0:T(8,128)(2,1)S(1)}, bf16[1,2,128,128]{3,2,1,0:T(8,128)(2,1)}, u32[]{:S(2)}, u32[]{:S(2)}) collective-permute-start(bf16[1,2,128,128]{3,2,1,0:T(8,128)(2,1)S(1)} %get-tuple-element.437), channel_id=1, source_target_pairs={{2,0},{4,2},{6,4},{0,6},{3,1},{5,3},{7,5},{1,7},{10,8},{12,10},{14... | collective-permute-start | bytes 196616 | tf_op jit(solution)/shard_map/ppermute | solution.py:30
  227.3 14.0 %collective-permute-start.16 = (bf16[1,2,128,128]{3,2,1,0:T(8,128)(2,1)S(1)}, bf16[1,2,128,128]{3,2,1,0:T(8,128)(2,1)}, u32[]{:S(2)}, u32[]{:S(2)}) collective-permute-start(bf16[1,2,128,128]{3,2,1,0:T(8,128)(2,1)S(1)} %get-tuple-element.436), channel_id=1, source_target_pairs={{0,1},{1,0},{2,3},{3,2},{4,5},{5,4},{6,7},{7,6},{8,9},{9,8},{10,11... | collective-permute-start | bytes 196616 | tf_op jit(solution)/shard_map/ppermute | solution.py:28
  230.7 18.2 %copy-start.6 = (f32[1,2048,128]{2,1,0:T(8,128)S(1)}, f32[1,2048,128]{2,1,0:T(8,128)}, u32[]{:S(2)}) copy-start(f32[1,2048,128]{2,1,0:T(8,128)} %subtract_divide_fusion.1) | copy-start | bytes 3145732
  237.1 54.6 %copy-start.9 = (f32[3]{0:T(128)S(1)}, f32[3]{0:T(128)}, u32[]{:S(2)}) copy-start(f32[3]{0:T(128)} %constant.255.clone.1) | copy-start | bytes 40
  238.1 4.3 %collective-permute-start.17 = (bf16[1,2,128,128]{3,2,1,0:T(8,128)(2,1)S(1)}, bf16[1,2,128,128]{3,2,1,0:T(8,128)(2,1)S(1)}, u32[]{:S(2)}, u32[]{:S(2)}) collective-permute-start(bf16[1,2,128,128]{3,2,1,0:T(8,128)(2,1)S(1)} %get-tuple-element.436), channel_id=1, source_target_pairs={{1,0},{0,1},{3,2},{2,3},{5,4},{4,5},{7,6},{6,7},{9,8},{8,9},{11,10... | collective-permute-start | bytes 196616 | tf_op jit(solution)/shard_map/ppermute | solution.py:30
  (4 other events, 44.3 us)
